TPU v7x, 256 devices: a whole 4x4x8 slice. The times are simulated.
256 devices in a mesh: tok: 8 (over x, core), hid: 32 (over y, z).
Axes of the slice: x: 4, y: 4, z: 8, core: 2. Of those that a mesh axis runs over, the one named last changes fastest.
Arguments:
- layer_input: bfloat16 [6144, 5120], P(('tok', 'hid')), may hold values from -6 to 6
- output_grad: bfloat16 [6144, 5120], P(('tok', 'hid')), may hold values from -6 to 6
- gate_weight: bfloat16 [5120, 8192], P(None, 'hid'), may hold values from -0.078125 to 0.078125
- up_weight: bfloat16 [5120, 8192], P(None, 'hid'), may hold values from -0.078125 to 0.078125
- down_weight: bfloat16 [8192, 5120], P('hid'), may hold values from -0.0625 to 0.0625
- block_lists: int32 [48, 32], P('tok'), may hold values from 0 to 63, as said below
- block_count: int32 [48], P('tok'), may hold values from 8 to 32, as said below
Outputs:
- input_grad: bfloat16 [6144, 5120], P(('tok', 'hid'))
- gate_grad: bfloat16 [5120, 8192], P('tok', 'hid')
- up_grad: bfloat16 [5120, 8192], P('tok', 'hid')
- down_grad: bfloat16 [8192, 5120], P('hid', 'tok')
Inputs may be any that keep to these rules, and one draw needn't show every extreme that they name: Each row of block_lists holds 32 different block numbers; entries past the tile's count are valid block numbers too and are not active. `block_count`: some tile uses all 32 slots and some tile uses 8.
All inputs are finite; a program needn't handle non-finite values.
Results may differ from a plain program's by a relative error of at most 0.015.
Values may be sent and summed in bfloat16 or wider, within the bound.
No kernel may reach another device: no remote copies, remote signals or barrier semaphores. Data moves between devices by JAX's collectives and lax.ppermute only.
A program may use at most 128 MiB of HBM per device.

v0:
```python
import math

import jax
import jax.numpy as jnp
from jax import lax
from jax.sharding import PartitionSpec as P

BLOCK = 128
TILE = 128


def tile_activity(block_lists, block_count, local_blocks):
    in_list = jnp.arange(block_lists.shape[1])[None, :] < block_count[:, None]
    hits = (block_lists[:, :, None] == local_blocks[None, None, :]) & in_list[:, :, None]
    return jnp.any(hits, axis=1)


def unit_grads(gate_pre, up_pre, grad_hidden, unit_mask):
    sigmoid_g = jax.nn.sigmoid(gate_pre)
    silu_g = gate_pre * sigmoid_g
    hidden = (unit_mask * silu_g * up_pre).astype(jnp.bfloat16)
    grad_gate = (
        unit_mask * grad_hidden * up_pre * sigmoid_g * (1.0 + gate_pre * (1.0 - sigmoid_g))
    ).astype(jnp.bfloat16)
    grad_up = (unit_mask * grad_hidden * silu_g).astype(jnp.bfloat16)
    return (hidden, grad_gate, grad_up)


def body(layer_input, output_grad, gate_weight, up_weight, down_weight, block_lists, block_count):
    contract_last = (((1,), (1,)), ((), ()))
    contract_first = (((0,), (0,)), ((), ()))
    width = gate_weight.shape[1]
    blocks_here = width // BLOCK
    local_blocks = lax.axis_index("hid") * blocks_here + jnp.arange(blocks_here, dtype=jnp.int32)
    active = tile_activity(block_lists, block_count, local_blocks)
    inputs_full = lax.all_gather(layer_input, "hid", axis=0, tiled=True)
    grads_full = lax.all_gather(output_grad, "hid", axis=0, tiled=True)
    tok_rows = inputs_full.shape[0]
    tiles_here = tok_rows // TILE
    unit_mask = jnp.broadcast_to(
        active.astype(jnp.float32)[:, None, :, None], (tiles_here, TILE, blocks_here, BLOCK)
    ).reshape(tok_rows, width)
    gate_pre = jnp.dot(inputs_full, gate_weight, preferred_element_type=jnp.float32)
    up_pre = jnp.dot(inputs_full, up_weight, preferred_element_type=jnp.float32)
    grad_hidden = lax.dot_general(
        grads_full, down_weight, contract_last, preferred_element_type=jnp.float32
    )
    hidden, grad_gate, grad_up = unit_grads(gate_pre, up_pre, grad_hidden, unit_mask)
    total = lax.dot_general(
        grad_gate, gate_weight, contract_last, preferred_element_type=jnp.float32
    )
    input_grad = lax.psum_scatter(
        (
            total
            + lax.dot_general(grad_up, up_weight, contract_last, preferred_element_type=jnp.float32)
        ).astype(jnp.bfloat16),
        "hid",
        scatter_dimension=0,
        tiled=True,
    )
    scale = 1.0 / math.sqrt(tok_rows * lax.axis_size("tok"))
    term_gate = lax.dot_general(
        inputs_full, grad_gate, contract_first, preferred_element_type=jnp.float32
    )
    term_up = lax.dot_general(
        inputs_full, grad_up, contract_first, preferred_element_type=jnp.float32
    )
    term_down = lax.dot_general(
        grads_full, hidden, contract_first, preferred_element_type=jnp.float32
    )
    stacked = lax.psum_scatter(
        (jnp.concatenate([term_gate, term_up, term_down], axis=1) * scale).astype(jnp.bfloat16),
        "tok",
        scatter_dimension=0,
        tiled=True,
    ).astype(jnp.float32)
    gate_grad = stacked[:, :width].astype(jnp.bfloat16)
    up_grad = stacked[:, width : 2 * width].astype(jnp.bfloat16)
    down_grad = stacked[:, 2 * width :].T.astype(jnp.bfloat16)
    return (input_grad, gate_grad, up_grad, down_grad)


def solution(mesh):
    in_specs = (
        P(("tok", "hid"), None),
        P(("tok", "hid"), None),
        P(None, "hid"),
        P(None, "hid"),
        P("hid", None),
        P("tok", None),
        P("tok"),
    )
    out_specs = (P(("tok", "hid"), None), P("tok", "hid"), P("tok", "hid"), P("hid", "tok"))
    return jax.shard_map(body, mesh=mesh, in_specs=in_specs, out_specs=out_specs, check_vma=False)
```

profile of v0, /device:TPU:2, one launch (start us, length us, event | category | flops | bytes accessed | tf_op | source)
XLA Modules:
  0.0 524.5 jit_solution(14032201681853211890)
XLA Ops:
  7.2 0.0 copy-start
  7.2 0.0 all-gather.5.cloned.1.call-start
  7.2 0.7 all-gather.5.cloned.1.call-update
  7.9 0.0 all-gather.3.cloned.1.call-start
  8.0 0.7 all-gather.3.cloned.1.call-update
  8.7 0.0 reduce-scatter.7.cloned.1.call-start
  8.7 0.7 iota_compare_fusion
  9.5 0.9 and_reduce_fusion
  10.4 0.1 copy.15
  10.5 98.3 %all-gather.5.cloned.1.call-done = bf16[768,5120]{1,0:T(8,128)(2,1)} async-done(((bf16[24,5120]{1,0:T(8,128)(2,1)}), bf16[768,5120]{1,0:T(8,128)(2,1)}) %all-gather.5.cloned.1.call-update) | async-done | bytes 7864336 | tf_op jit(solution)/shard_map/all_gather | solution.py:36
  108.8 0.0 copy-done
  108.8 0.0 copy-start.1
  108.8 0.0 copy-start.2
  108.8 5.6 %fusion.9 = f32[768,256]{1,0:T(8,128)S(1)} fusion(bf16[768,5120]{1,0:T(8,128)(2,1)} %all-gather.5.cloned.1.call-done, bf16[5120,256]{1,0:T(8,128)(2,1)S(1)} %copy-done), kind=kOutput, calls=%fused_computation.20 | convolution fusion | flops 2013265920 | bytes 11272192 | tf_op jit(solution)/shard_map/dot_general | solution.py:43
  114.4 0.0 copy-done.1
  114.4 0.6 copy-done.2
  115.0 3.1 fusion.8
  118.1 85.6 %all-gather.3.cloned.1.call-done = bf16[768,5120]{1,0:T(8,128)(2,1)} async-done(((bf16[24,5120]{1,0:T(8,128)(2,1)}), bf16[768,5120]{1,0:T(8,128)(2,1)}) %all-gather.3.cloned.1.call-update) | async-done | bytes 7864336 | tf_op jit(solution)/shard_map/all_gather | solution.py:37
  203.7 0.0 slice-start.2
  203.7 0.3 broadcast_in_dim.2
  203.9 0.0 copy-done.4
  204.0 0.0 slice-start.3
  204.0 0.0 copy-start.5
  204.0 0.0 copy-start.6
  204.0 0.0 slice-start
  204.0 6.1 %convolution_bitcast_fusion = f32[5120,256]{0,1:T(8,128)S(1)} fusion(bf16[768,5120]{1,0:T(8,128)(2,1)} %all-gather.3.cloned.1.call-done, f32[768,256]{1,0:T(8,128)} %fusion.8, f32[96,8,2,128]{3,2,1,0:T(2,128)S(1)} %bitcast.37, f32[768,256]{1,0:T(8,128)S(1)} %fusion.9), kind=kOutput, calls=%fused_computation.3 | convolution fusion | flops 2014642176 | bytes 15466496 | tf_op jit(solution)/shard_map/dot_general | solution.py:68
  210.1 0.0 slice-done.2
  210.1 0.0 slice-done.3
  210.2 0.0 copy-done.5
  210.2 0.3 copy-done.6
  210.5 3.7 multiply_convert_fusion
  214.3 0.0 slice-done
  214.3 0.0 slice-done.1
  214.3 2.2 convolution_bitcast_fusion.1
  216.5 2.4 convolution_bitcast_fusion.2
  219.0 4.4 fusion
  223.3 10.6 %copy.18 = bf16[5120,768]{1,0:T(8,128)(2,1)} copy(bf16[5120,768]{0,1:T(8,128)(2,1)} %fusion) | data formatting | bytes 15728640
  233.9 0.0 reduce-scatter.7.cloned.1.call-update
  234.0 0.0 reduce-scatter.5.cloned.1.call-start
  234.0 0.0 copy-start.3
  234.0 7.7 %fusion.10 = f32[768,5120]{1,0:T(8,128)} fusion(bf16[768,256]{1,0:T(8,128)(2,1)S(1)} %get-tuple-element.17, bf16[5120,256]{1,0:T(8,128)(2,1)S(1)} %copy-done), kind=kOutput, calls=%fused_computation.21 | convolution fusion | flops 2013265920 | bytes 18743296 | tf_op jit(solution)/shard_map/dot_general | solution.py:49
  241.8 0.0 copy-done.3
  241.8 11.8 %add_convert_fusion = bf16[768,5120]{1,0:T(8,128)(2,1)} fusion(f32[768,5120]{1,0:T(8,128)} %fusion.10, bf16[768,256]{1,0:T(8,128)(2,1)S(1)} %get-tuple-element.16, bf16[5120,256]{1,0:T(8,128)(2,1)S(1)} %copy-done.3), kind=kOutput, calls=%fused_computation.2 | convolution fusion | flops 2021130240 | bytes 26607616 | tf_op jit(solution)/shard_map/dot_general | solution.py:55
  253.5 0.0 reduce-scatter.5.cloned.1.call-update
  253.6 27.8 %reduce-scatter.7.cloned.1.call-done = bf16[640,768]{1,0:T(8,128)(2,1)} async-done(((bf16[5120,768]{1,0:T(8,128)(2,1)}), bf16[640,768]{1,0:T(8,128)(2,1)}) %reduce-scatter.7.cloned.1.call-update) | async-done | bytes 983056
  281.4 2.1 fusion.7
  283.4 0.9 copy.22
  284.3 233.7 %reduce-scatter.5.cloned.1.call-done = bf16[24,5120]{1,0:T(8,128)(2,1)} async-done(((bf16[768,5120]{1,0:T(8,128)(2,1)}), bf16[24,5120]{1,0:T(8,128)(2,1)}) %reduce-scatter.5.cloned.1.call-update) | async-done | bytes 245776 | tf_op jit(solution)/shard_map/reduce_scatter | solution.py:52
  (6 shorter events, 0.0 us)
Async XLA Ops:
  7.2 101.6 %copy-start = (bf16[5120,256]{1,0:T(8,128)(2,1)S(1)}, bf16[5120,256]{1,0:T(8,128)(2,1)}, u32[]{:S(2)}) copy-start(bf16[5120,256]{1,0:T(8,128)(2,1)} %param.9) | copy-start | bytes 7864324
  7.2 101.6 %all-gather.5.cloned.1.call-start = ((), (), s32[]{:S(2)}) async-start(), calls=%async_computation.3 | async-start | bytes 8110080 | tf_op jit(solution)/shard_map/all_gather | solution.py:36
  7.9 195.8 %all-gather.3.cloned.1.call-start = ((), (), s32[]{:S(2)}) async-start(), calls=%async_computation.2 | async-start | bytes 8110080 | tf_op jit(solution)/shard_map/all_gather | solution.py:37
  8.7 272.7 %reduce-scatter.7.cloned.1.call-start = ((), (), s32[]{:S(2)}) async-start(), calls=%async_computation.5 | async-start | bytes 8847360
  108.8 5.6 %copy-start.1 = (bf16[768,5120]{1,0:T(8,128)(2,1)S(1)}, bf16[768,5120]{1,0:T(8,128)(2,1)}, u32[]{:S(2)}) copy-start(bf16[768,5120]{1,0:T(8,128)(2,1)} %all-gather.5.cloned.1.call-done) | copy-start | bytes 23592964
  108.8 6.2 %copy-start.2 = (bf16[5120,256]{1,0:T(8,128)(2,1)S(1)}, bf16[5120,256]{1,0:T(8,128)(2,1)}, u32[]{:S(2)}) copy-start(bf16[5120,256]{1,0:T(8,128)(2,1)} %param.10) | copy-start | bytes 7864324
  115.0 89.0 %copy-start.4 = (f32[768,256]{1,0:T(8,128)}, f32[768,256]{1,0:T(8,128)S(1)}, u32[]{:S(2)}) copy-start(f32[768,256]{1,0:T(8,128)S(1)} %fusion.9) | copy-start | bytes 2359300
  203.7 6.5 %slice-start.2 = ((s8[7864320]{0:T(1024)(128)(4,1)}), s8[4194304]{0:T(1024)(128)(4,1)S(1)}, s32[]{:S(2)}) async-start(s8[7864320]{0:T(1024)(128)(4,1)} %bitcast.35), calls=%async_computation.8 | async-start | bytes 8388608
  204.0 6.2 %slice-start.3 = ((s8[7864320]{0:T(1024)(128)(4,1)}), s8[3670016]{0:T(1024)(128)(4,1)S(1)}, s32[]{:S(2)}) async-start(s8[7864320]{0:T(1024)(128)(4,1)} %bitcast.35), calls=%async_computation.9 | async-start | bytes 7340032
  204.0 6.2 %copy-start.5 = (f32[768,256]{1,0:T(8,128)S(1)}, f32[768,256]{1,0:T(8,128)}, u32[]{:S(2)}) copy-start(f32[768,256]{1,0:T(8,128)} %fusion.8) | copy-start | bytes 2359300
  204.0 6.5 %copy-start.6 = (bf16[256,5120]{1,0:T(8,128)(2,1)S(1)}, bf16[256,5120]{1,0:T(8,128)(2,1)}, u32[]{:S(2)}) copy-start(bf16[256,5120]{1,0:T(8,128)(2,1)} %param.11) | copy-start | bytes 7864324
  204.0 10.3 %slice-start = ((s8[7864320]{0:T(1024)(128)(4,1)}), s8[4194304]{0:T(1024)(128)(4,1)S(1)}, s32[]{:S(2)}) async-start(s8[7864320]{0:T(1024)(128)(4,1)} %bitcast.33), calls=%async_computation.6 | async-start | bytes 8388608
  210.5 3.8 slice-start.1
  234.0 284.0 %reduce-scatter.5.cloned.1.call-start = ((), (), s32[]{:S(2)}) async-start(), calls=%async_computation.4 | async-start | bytes 8110080 | tf_op jit(solution)/shard_map/reduce_scatter | solution.py:52
  234.0 7.8 %copy-start.3 = (bf16[5120,256]{1,0:T(8,128)(2,1)S(1)}, bf16[5120,256]{1,0:T(8,128)(2,1)}, u32[]{:S(2)}) copy-start(bf16[5120,256]{1,0:T(8,128)(2,1)} %param.10) | copy-start | bytes 7864324
Sparse Core Ops, SparseCore 0:
  10.6 98.1 all-gather.4
  111.3 92.2 all-gather.2
  234.1 47.2 reduce-scatter.6
  285.8 232.1 reduce-scatter.4
where the time goes:
time: 525 us
  waiting for transfers between devices  447 us (85%)
  matrix products  42.7 us (8%)
  local copies, waits for them, and re-layouts  15 us (3%)
  between operations  13.9 us (3%)
  other arithmetic  6.01 us (1%)
    reduce_scatter x1, waiting for transfers between devices, body(): lax.psum_scatter((total + lax.dot_general(grad_up, up_weight, contract_la...  234 us
    all_gather x1, waiting for transfers between devices, body(): inputs_full = lax.all_gather(layer_input, 'hid', axis=0, tiled=True)  98.3 us
    all_gather x1, waiting for transfers between devices, body(): grads_full = lax.all_gather(output_grad, 'hid', axis=0, tiled=True)  85.6 us
    unnamed x5, waiting for transfers between devices  29.2 us
    unnamed x24, local copies, waits for them, and re-layouts  12.5 us
    dot_general x1, matrix products, body(): lax.dot_general(grad_up, up_weight, contract_last, preferred_element_type...  11.8 us
  transfers between devices with their start and end apart: 4, of which 4 were waited for; matrix products, arithmetic and copies ran while one was open for 6% of the time, Pallas kernels for 0%

commit v1 on v0

--- a/solution.py
+++ b/solution.py
@@ -3,10 +3,19 @@
 import jax
 import jax.numpy as jnp
 from jax import lax
-from jax.sharding import PartitionSpec as P
+from jax.sharding import Mesh, PartitionSpec as P
 
 BLOCK = 128
 TILE = 128
+
+
+def to_tiles(a):
+    r, c = a.shape
+    return a.reshape(r // 8, 8, c // 128, 128).transpose(0, 2, 1, 3).reshape(r * c // 128, 128)
+
+
+def from_tiles(a, r, c):
+    return a.reshape(r // 8, c // 128, 8, 128).transpose(0, 2, 1, 3).reshape(r, c)
 
 
 def tile_activity(block_lists, block_count, local_blocks):
@@ -29,13 +38,14 @@
 def body(layer_input, output_grad, gate_weight, up_weight, down_weight, block_lists, block_count):
     contract_last = (((1,), (1,)), ((), ()))
     contract_first = (((0,), (0,)), ((), ()))
+    rows, d_model = layer_input.shape
     width = gate_weight.shape[1]
     blocks_here = width // BLOCK
     local_blocks = lax.axis_index("hid") * blocks_here + jnp.arange(blocks_here, dtype=jnp.int32)
     active = tile_activity(block_lists, block_count, local_blocks)
-    inputs_full = lax.all_gather(layer_input, "hid", axis=0, tiled=True)
-    grads_full = lax.all_gather(output_grad, "hid", axis=0, tiled=True)
-    tok_rows = inputs_full.shape[0]
+    tok_rows = rows * lax.axis_size("hid")
+    inputs_full = from_tiles(lax.all_gather(to_tiles(layer_input), "hid", axis=0, tiled=True), tok_rows, d_model)
+    grads_full = from_tiles(lax.all_gather(to_tiles(output_grad), "hid", axis=0, tiled=True), tok_rows, d_model)
     tiles_here = tok_rows // TILE
     unit_mask = jnp.broadcast_to(
         active.astype(jnp.float32)[:, None, :, None], (tiles_here, TILE, blocks_here, BLOCK)
@@ -49,14 +59,12 @@
     total = lax.dot_general(
         grad_gate, gate_weight, contract_last, preferred_element_type=jnp.float32
     )
-    input_grad = lax.psum_scatter(
-        (
-            total
-            + lax.dot_general(grad_up, up_weight, contract_last, preferred_element_type=jnp.float32)
-        ).astype(jnp.bfloat16),
-        "hid",
-        scatter_dimension=0,
-        tiled=True,
+    partial = (
+        total
+        + lax.dot_general(grad_up, up_weight, contract_last, preferred_element_type=jnp.float32)
+    ).astype(jnp.bfloat16)
+    input_grad = from_tiles(
+        lax.psum_scatter(to_tiles(partial), "hid", scatter_dimension=0, tiled=True), rows, d_model
     )
     scale = 1.0 / math.sqrt(tok_rows * lax.axis_size("tok"))
     term_gate = lax.dot_general(

time: 525 us -> 525 us (level)
    unnamed x24 -> x26, local copies, waits for them, and re-layouts: 12.5 us -> 12.6 us
where the time goes in v1:
time: 525 us
  waiting for transfers between devices  447 us (85%)
  matrix products  42.7 us (8%)
  local copies, waits for them, and re-layouts  15 us (3%)
  between operations  14 us (3%)
  other arithmetic  6.04 us (1%)
    reduce_scatter x1, waiting for transfers between devices, body(): lax.psum_scatter(to_tiles(partial), 'hid', scatter_dimension=0, tiled=True)  234 us
    all_gather x1, waiting for transfers between devices, body(): lax.all_gather(to_tiles(layer_input), 'hid', axis=0, tiled=True)  98.3 us
    all_gather x1, waiting for transfers between devices, body(): lax.all_gather(to_tiles(output_grad), 'hid', axis=0, tiled=True)  85.5 us
    unnamed x5, waiting for transfers between devices  29.2 us
    unnamed x26, local copies, waits for them, and re-layouts  12.6 us
    dot_general x1, matrix products, body(): lax.dot_general(grad_up, up_weight, contract_last, preferred_element_type...  11.8 us
  transfers between devices with their start and end apart: 4, of which 4 were waited for; matrix products, arithmetic and copies ran while one was open for 6% of the time, Pallas kernels for 0%

profile of v1, /device:TPU:2, one launch (start us, length us, event | category | flops | bytes accessed | tf_op | source)
XLA Modules:
  0.0 524.6 jit_solution(17337344538193097124)
XLA Ops:
  7.2 0.0 copy-start
  7.2 0.0 all-gather.5.cloned.1.call-start
  7.2 0.7 all-gather.5.cloned.1.call-update
  7.9 0.0 all-gather.3.cloned.1.call-start
  8.0 0.7 all-gather.3.cloned.1.call-update
  8.7 0.0 reduce-scatter.7.cloned.1.call-start
  8.7 0.7 iota_compare_fusion
  9.5 0.9 and_reduce_fusion
  10.4 0.1 copy.15
  10.5 98.3 %all-gather.5.cloned.1.call-done = bf16[30720,128]{1,0:T(8,128)(2,1)} async-done(((bf16[960,128]{1,0:T(8,128)(2,1)}), bf16[30720,128]{1,0:T(8,128)(2,1)}) %all-gather.5.cloned.1.call-update) | async-done | bytes 7864336 | tf_op jit(solution)/shard_map/all_gather | solution.py:47
  108.8 0.0 slice-start
  108.8 0.0 copy-start.1
  108.8 0.0 copy-done
  108.8 5.6 %fusion.9 = f32[768,256]{1,0:T(8,128)S(1)} fusion(bf16[768,5120]{1,0:T(8,128)(2,1)} %bitcast.63, bf16[5120,256]{1,0:T(8,128)(2,1)S(1)} %copy-done), kind=kOutput, calls=%fused_computation.20 | convolution fusion | flops 2013265920 | bytes 11272192 | tf_op jit(solution)/shard_map/dot_general | solution.py:53
  114.4 0.0 slice-done
  114.4 0.0 copy-done.1
  114.4 0.7 slice-done.1
  115.1 3.1 fusion.8
  118.2 85.5 %all-gather.3.cloned.1.call-done = bf16[30720,128]{1,0:T(8,128)(2,1)} async-done(((bf16[960,128]{1,0:T(8,128)(2,1)}), bf16[30720,128]{1,0:T(8,128)(2,1)}) %all-gather.3.cloned.1.call-update) | async-done | bytes 7864336 | tf_op jit(solution)/shard_map/all_gather | solution.py:48
  203.7 0.3 broadcast_in_dim.2
  203.9 0.0 copy-done.3
  204.0 0.0 slice-start.5
  204.0 0.0 copy-start.4
  204.0 0.0 copy-start.5
  204.0 0.0 slice-start.2
  204.0 6.1 %convolution_bitcast_fusion = f32[5120,256]{0,1:T(8,128)S(1)} fusion(bf16[768,5120]{1,0:T(8,128)(2,1)} %bitcast.72, f32[768,256]{1,0:T(8,128)} %fusion.8, f32[96,8,2,128]{3,2,1,0:T(2,128)S(1)} %bitcast.76, f32[768,256]{1,0:T(8,128)S(1)} %fusion.9), kind=kOutput, calls=%fused_computation.3 | convolution fusion | flops 2014642176 | bytes 15466496 | tf_op jit(solution)/shard_map/dot_general | solution.py:76
  210.1 0.0 slice-done.4
  210.1 0.0 slice-done.5
  210.2 0.0 copy-done.4
  210.2 0.3 copy-done.5
  210.5 3.7 multiply_convert_fusion
  214.3 0.0 slice-done.2
  214.3 0.0 slice-done.3
  214.3 2.2 convolution_bitcast_fusion.1
  216.5 2.4 convolution_bitcast_fusion.2
  218.9 4.4 fusion
  223.4 10.6 %copy.18 = bf16[5120,768]{1,0:T(8,128)(2,1)} copy(bf16[5120,768]{0,1:T(8,128)(2,1)} %fusion) | data formatting | bytes 15728640
  234.0 0.0 reduce-scatter.7.cloned.1.call-update
  234.0 0.0 reduce-scatter.5.cloned.1.call-start
  234.1 0.0 copy-start.2
  234.1 7.7 %fusion.10 = f32[768,5120]{1,0:T(8,128)} fusion(bf16[768,256]{1,0:T(8,128)(2,1)S(1)} %get-tuple-element.17, bf16[5120,256]{1,0:T(8,128)(2,1)S(1)} %copy-done), kind=kOutput, calls=%fused_computation.21 | convolution fusion | flops 2013265920 | bytes 18743296 | tf_op jit(solution)/shard_map/dot_general | solution.py:59
  241.8 0.0 copy-done.2
  241.8 11.8 %add_convert_fusion = bf16[768,5120]{1,0:T(8,128)(2,1)} fusion(f32[768,5120]{1,0:T(8,128)} %fusion.10, bf16[768,256]{1,0:T(8,128)(2,1)S(1)} %get-tuple-element.16, bf16[5120,256]{1,0:T(8,128)(2,1)S(1)} %copy-done.2), kind=kOutput, calls=%fused_computation.2 | convolution fusion | flops 2021130240 | bytes 26607616 | tf_op jit(solution)/shard_map/dot_general | solution.py:64
  253.6 0.0 reduce-scatter.5.cloned.1.call-update
  253.6 27.8 %reduce-scatter.7.cloned.1.call-done = bf16[640,768]{1,0:T(8,128)(2,1)} async-done(((bf16[5120,768]{1,0:T(8,128)(2,1)}), bf16[640,768]{1,0:T(8,128)(2,1)}) %reduce-scatter.7.cloned.1.call-update) | async-done | bytes 983056
  281.4 2.1 fusion.7
  283.5 0.9 copy.22
  284.4 233.7 %reduce-scatter.5.cloned.1.call-done = bf16[960,128]{1,0:T(8,128)(2,1)} async-done(((bf16[30720,128]{1,0:T(8,128)(2,1)}), bf16[960,128]{1,0:T(8,128)(2,1)}) %reduce-scatter.5.cloned.1.call-update) | async-done | bytes 245776 | tf_op jit(solution)/shard_map/reduce_scatter | solution.py:67
  (9 shorter events, 0.0 us)
Async XLA Ops:
  7.2 101.6 %copy-start = (bf16[5120,256]{1,0:T(8,128)(2,1)S(1)}, bf16[5120,256]{1,0:T(8,128)(2,1)}, u32[]{:S(2)}) copy-start(bf16[5120,256]{1,0:T(8,128)(2,1)} %param.9) | copy-start | bytes 7864324
  7.2 101.6 %all-gather.5.cloned.1.call-start = ((), (), s32[]{:S(2)}) async-start(), calls=%async_computation.3 | async-start | bytes 8110080 | tf_op jit(solution)/shard_map/all_gather | solution.py:47
  7.9 195.8 %all-gather.3.cloned.1.call-start = ((), (), s32[]{:S(2)}) async-start(), calls=%async_computation.2 | async-start | bytes 8110080 | tf_op jit(solution)/shard_map/all_gather | solution.py:48
  8.7 272.7 %reduce-scatter.7.cloned.1.call-start = ((), (), s32[]{:S(2)}) async-start(), calls=%async_computation.5 | async-start | bytes 8847360
  108.8 5.6 %slice-start = ((s8[7864320]{0:T(1024)(128)(4,1)}), s8[4194304]{0:T(1024)(128)(4,1)S(1)}, s32[]{:S(2)}) async-start(s8[7864320]{0:T(1024)(128)(4,1)} %bitcast.64), calls=%async_computation.6 | async-start | bytes 8388608
  108.8 5.6 %copy-start.1 = (bf16[5120,256]{1,0:T(8,128)(2,1)S(1)}, bf16[5120,256]{1,0:T(8,128)(2,1)}, u32[]{:S(2)}) copy-start(bf16[5120,256]{1,0:T(8,128)(2,1)} %param.10) | copy-start | bytes 7864324
  108.8 6.3 %slice-start.1 = ((s8[7864320]{0:T(1024)(128)(4,1)}), s8[3670016]{0:T(1024)(128)(4,1)S(1)}, s32[]{:S(2)}) async-start(s8[7864320]{0:T(1024)(128)(4,1)} %bitcast.64), calls=%async_computation.7 | async-start | bytes 7340032
  115.1 88.9 %copy-start.3 = (f32[768,256]{1,0:T(8,128)}, f32[768,256]{1,0:T(8,128)S(1)}, u32[]{:S(2)}) copy-start(f32[768,256]{1,0:T(8,128)S(1)} %fusion.9) | copy-start | bytes 2359300
  203.7 6.5 %slice-start.4 = ((s8[7864320]{0:T(1024)(128)(4,1)}), s8[4194304]{0:T(1024)(128)(4,1)S(1)}, s32[]{:S(2)}) async-start(s8[7864320]{0:T(1024)(128)(4,1)} %bitcast.73), calls=%async_computation.10 | async-start | bytes 8388608
  204.0 6.2 %slice-start.5 = ((s8[7864320]{0:T(1024)(128)(4,1)}), s8[3670016]{0:T(1024)(128)(4,1)S(1)}, s32[]{:S(2)}) async-start(s8[7864320]{0:T(1024)(128)(4,1)} %bitcast.73), calls=%async_computation.11 | async-start | bytes 7340032
  204.0 6.2 %copy-start.4 = (f32[768,256]{1,0:T(8,128)S(1)}, f32[768,256]{1,0:T(8,128)}, u32[]{:S(2)}) copy-start(f32[768,256]{1,0:T(8,128)} %fusion.8) | copy-start | bytes 2359300
  204.0 6.5 %copy-start.5 = (bf16[256,5120]{1,0:T(8,128)(2,1)S(1)}, bf16[256,5120]{1,0:T(8,128)(2,1)}, u32[]{:S(2)}) copy-start(bf16[256,5120]{1,0:T(8,128)(2,1)} %param.11) | copy-start | bytes 7864324
  204.0 10.3 %slice-start.2 = ((s8[7864320]{0:T(1024)(128)(4,1)}), s8[4194304]{0:T(1024)(128)(4,1)S(1)}, s32[]{:S(2)}) async-start(s8[7864320]{0:T(1024)(128)(4,1)} %bitcast.67), calls=%async_computation.8 | async-start | bytes 8388608
  210.5 3.8 slice-start.3
  234.0 284.0 %reduce-scatter.5.cloned.1.call-start = ((), (), s32[]{:S(2)}) async-start(), calls=%async_computation.4 | async-start | bytes 8110080 | tf_op jit(solution)/shard_map/reduce_scatter | solution.py:67
  234.1 7.7 %copy-start.2 = (bf16[5120,256]{1,0:T(8,128)(2,1)S(1)}, bf16[5120,256]{1,0:T(8,128)(2,1)}, u32[]{:S(2)}) copy-start(bf16[5120,256]{1,0:T(8,128)(2,1)} %param.10) | copy-start | bytes 7864324
Sparse Core Ops, SparseCore 0:
  10.6 98.1 all-gather.4
  111.3 92.2 all-gather.2
  234.1 47.2 reduce-scatter.6
  285.9 232.1 reduce-scatter.4
